TPU v7x, 512 devices: a whole 4x8x8 slice. The times are simulated.
512 devices in a mesh: row: 32 (over y, x), col: 16 (over z, core).
Axes of the slice: x: 4, y: 8, z: 8, core: 2. Of those that a mesh axis runs over, the one named last changes fastest.
Arguments:
- blocks: bfloat16 [32, 16, 2, 8, 128, 128], P('row', 'col'), may hold values from -4 to 4
- block_rows: int32 [32, 16, 2, 8], P('row', 'col'), may hold values from 0 to 4, as said below
- block_cols: int32 [32, 16, 2, 8], P('row', 'col'), may hold values from 0 to 4, as said below
- counts: int32 [32, 16, 2], P('row', 'col'), may hold values from 2 to 8, as said below
Outputs:
- square: bfloat16 [20480, 20480], P('row', 'col')
- trace_value: float32 [], replicated
Inputs may be any that keep to these rules, and one draw needn't show every extreme that they name: `block_rows`: in every (row panel, column panel, group) the 8 slots name distinct block positions; a slot holds data only if its index is below the group's count. `block_cols`: together with block_rows each slot names a distinct position of the 5 x 5 grid of its group. `counts`: some group is full in every draw.
All inputs are finite; a program needn't handle non-finite values.
Results may differ from a plain program's by a relative error of at most 0.001.
Values may be sent and summed in bfloat16 or wider, within the bound.
A program may use at most 64 MiB of HBM per device.

v0:
```python
import math
import jax
import jax.numpy as jnp
from jax import lax
from jax.sharding import PartitionSpec as P

RB = 5
STEPS = 4


def as_sent(shard):
    return jax.tree.map(lambda a: a.astype(jnp.bfloat16) if a.dtype == jnp.float32 else a, shard)


def passed_along(block, axis, distance):
    devices = range(lax.axis_size(axis))
    route = [((i - distance) % len(devices), i) for i in devices]
    return lax.ppermute(block, axis, route)


def densify(pieces, rows, cols, nrows, ncols):
    width = pieces.shape[-1]
    count = pieces.shape[0]
    places = rows * ncols + cols
    onehot = (places[None, :] == jnp.arange(nrows * ncols, dtype=jnp.int32)[:, None]).astype(
        pieces.dtype
    )
    dense = jnp.dot(
        onehot, pieces.reshape(count, width * width), preferred_element_type=jnp.float32
    )
    dense = dense.reshape(nrows, ncols, width, width).transpose(0, 2, 1, 3)
    return dense.reshape(nrows * width, ncols * width).astype(pieces.dtype)


def pick(flag, kept, moved):
    return jax.tree.map(lambda first, second: jnp.where(flag, second, first), kept, moved)


def body(blocks, block_rows, block_cols, counts):
    groups = blocks.shape[2]
    slot_count = blocks.shape[3]
    width = blocks.shape[4]
    row_count = lax.axis_size("row")
    col_count = lax.axis_size("col")
    row_place = lax.axis_index("row")
    col_place = lax.axis_index("col")
    upper = row_place // groups
    lower = row_place % groups
    filled = counts[0, 0]
    live = jnp.arange(slot_count, dtype=jnp.int32)[None, :] < filled[:, None]
    masked = blocks[0, 0] * live[..., None, None].astype(blocks.dtype)
    rows_here = block_rows[0, 0]
    offsets = (jnp.arange(groups, dtype=jnp.int32) * RB)[:, None]
    cols_here = block_cols[0, 0] + offsets
    left_pieces = lax.dynamic_index_in_dim(masked, lower, 0, keepdims=False)
    left_rows = lax.dynamic_index_in_dim(rows_here, lower, 0, keepdims=False)
    left_cols = lax.dynamic_index_in_dim(block_cols[0, 0], lower, 0, keepdims=False)
    left = (left_pieces, left_rows, left_cols)
    right = (masked, rows_here, cols_here)
    left_move = (col_count - upper % col_count) % col_count
    for bit in range((col_count - 1).bit_length()):
        moved = jax.tree.map(
            lambda part, own: part.astype(own.dtype),
            passed_along(as_sent(left), "col", 1 << bit),
            left,
        )
        left = pick(left_move >> bit & 1 == 1, left, moved)
    right_move = (row_count - groups * col_place % row_count) % row_count
    for bit in range((row_count - 1).bit_length()):
        moved = jax.tree.map(
            lambda part, own: part.astype(own.dtype),
            passed_along(as_sent(right), "row", 1 << bit),
            right,
        )
        right = pick(right_move >> bit & 1 == 1, right, moved)
    totals = jnp.zeros((RB * width, groups * RB * width), jnp.float32)
    for step in range(STEPS):
        if step > 0:
            left = jax.tree.map(
                lambda part, own: part.astype(own.dtype),
                passed_along(as_sent(left), "col", col_count - 1),
                left,
            )
            right = jax.tree.map(
                lambda part, own: part.astype(own.dtype),
                passed_along(as_sent(right), "row", row_count - groups),
                right,
            )
        right_dense = densify(
            right[0].reshape(groups * slot_count, width, width),
            right[1].reshape(-1),
            right[2].reshape(-1),
            RB,
            groups * RB,
        )
        left_dense = densify(left[0], left[1], left[2], RB, RB)
        totals = totals + jnp.dot(left_dense, right_dense, preferred_element_type=jnp.float32)
    shift_amount = row_place - groups * col_place
    valid = (shift_amount >= 0) & (shift_amount < groups)
    start = jnp.clip(shift_amount, 0, groups - 1) * RB * width
    window = lax.dynamic_slice_in_dim(totals, start, RB * width, 1)
    term = jnp.where(valid, jnp.trace(window), jnp.zeros((), jnp.float32))
    overall = lax.psum(term, ("row", "col"))
    trace_value = overall / math.sqrt(row_count * RB * width)
    return (totals.astype(jnp.bfloat16), trace_value)


def solution(mesh):
    return jax.shard_map(
        body,
        mesh=mesh,
        in_specs=(
            P("row", "col", None, None, None, None),
            P("row", "col", None, None),
            P("row", "col", None, None),
            P("row", "col", None),
        ),
        out_specs=(P("row", "col"), P()),
        check_vma=False,
    )
```

profile of v0, /device:TPU:1, one launch (start us, length us, event | category | flops | bytes accessed | tf_op | source)
XLA Modules:
  0.0 380.4 jit_solution(16158533486816690697)
XLA Ops:
  0.6 4.1 %collective-permute-start.12 = (s32[2,8]{1,0:T(2,128)}, s32[2,8]{1,0:T(2,128)S(1)}, u32[]{:S(2)}, u32[]{:S(2)}) collective-permute-start(s32[2,8]{1,0:T(2,128)} %bitcast.239), channel_id=1, source_target_pairs={{496,0},{0,16},{16,32},{32,48},{48,64},{64,80},{80,96},{96,112},{1... | collective-permute-start | bytes 200 | tf_op jit(solution)/shard_map/ppermute | solution.py:18
  5.5 3.1 collective-permute-start.17
  10.5 2.8 collective-permute-start.22
  13.4 3.5 collective-permute-start.8
  20.2 2.5 collective-permute-start.4
  23.4 3.9 %collective-permute-done.4 = s32[8]{0:T(128)S(1)} collective-permute-done((s32[8]{0:T(128)S(1)}, s32[8]{0:T(128)S(1)}, u32[]{:S(2)}, u32[]{:S(2)}) %collective-permute-start.4) | collective-permute-done | bytes 64 | tf_op jit(solution)/shard_map/ppermute | solution.py:18
  29.9 2.3 collective-permute-start.5
  32.8 4.6 %collective-permute-start.13 = (s32[2,8]{1,0:T(2,128)S(1)}, s32[2,8]{1,0:T(2,128)S(1)}, u32[]{:S(2)}, u32[]{:S(2)}) collective-permute-start(s32[2,8]{1,0:T(2,128)S(1)} %broadcast_select_fusion.10), channel_id=1, source_target_pairs={{480,0},{496,16},{0,32},{16,48},{32,64},{48,80},{64,96},{80,112},{... | collective-permute-start | bytes 200 | tf_op jit(solution)/shard_map/ppermute | solution.py:18
  38.2 3.1 collective-permute-start.18
  41.4 6.2 %collective-permute-start.2 = (s32[8]{0:T(128)S(1)}, s32[8]{0:T(128)S(1)}, u32[]{:S(2)}, u32[]{:S(2)}) collective-permute-start(s32[8]{0:T(128)S(1)} %broadcast_select_fusion.22), channel_id=1, source_target_pairs={{12,0},{13,1},{14,2},{15,3},{0,4},{1,5},{2,6},{3,7},{4,8},{5,9},{6... | collective-permute-start | bytes 104 | tf_op jit(solution)/shard_map/ppermute | solution.py:18
  48.3 4.5 %collective-permute-start.6 = (s32[8]{0:T(128)S(1)}, s32[8]{0:T(128)S(1)}, u32[]{:S(2)}, u32[]{:S(2)}) collective-permute-start(s32[8]{0:T(128)S(1)} %broadcast_select_fusion.21), channel_id=1, source_target_pairs={{12,0},{13,1},{14,2},{15,3},{0,4},{1,5},{2,6},{3,7},{4,8},{5,9},{6... | collective-permute-start | bytes 104 | tf_op jit(solution)/shard_map/ppermute | solution.py:18
  54.7 7.5 %collective-permute-start.3 = (s32[8]{0:T(128)S(1)}, s32[8]{0:T(128)S(1)}, u32[]{:S(2)}, u32[]{:S(2)}) collective-permute-start(s32[8]{0:T(128)S(1)} %broadcast_select_fusion.24), channel_id=1, source_target_pairs={{8,0},{9,1},{10,2},{11,3},{12,4},{13,5},{14,6},{15,7},{0,8},{1,9},... | collective-permute-start | bytes 104 | tf_op jit(solution)/shard_map/ppermute | solution.py:18
  62.1 1.9 collective-permute-start.7
  64.1 3.2 collective-permute-start.14
  67.3 3.2 collective-permute-start.19
  70.6 7.6 %collective-permute-start.28 = (s32[8]{0:T(128)S(1)}, s32[8]{0:T(128)S(1)}, u32[]{:S(2)}, u32[]{:S(2)}) collective-permute-start(s32[8]{0:T(128)S(1)} %get-tuple-element.4), channel_id=1, source_target_pairs={{1,0},{2,1},{3,2},{4,3},{5,4},{6,5},{7,6},{8,7},{9,8},{10,9},{11,1... | collective-permute-start | bytes 104 | tf_op jit(solution)/shard_map/ppermute | solution.py:18
  79.5 2.5 collective-permute-done.27
  83.7 2.9 collective-permute-start.33
  86.6 4.5 %collective-permute-start.15 = (s32[2,8]{1,0:T(2,128)S(1)}, s32[2,8]{1,0:T(2,128)S(1)}, u32[]{:S(2)}, u32[]{:S(2)}) collective-permute-start(s32[2,8]{1,0:T(2,128)S(1)} %broadcast_select_fusion.14), channel_id=1, source_target_pairs={{384,0},{400,16},{416,32},{432,48},{448,64},{464,80},{480,96},{496... | collective-permute-start | bytes 200 | tf_op jit(solution)/shard_map/ppermute | solution.py:18
  91.1 2.4 collective-permute-start.20
  94.2 2.4 collective-permute-done.40
  96.6 3.0 collective-permute-done.39
  99.5 4.4 %collective-permute-start.16 = (s32[2,8]{1,0:T(2,128)S(1)}, s32[2,8]{1,0:T(2,128)S(1)}, u32[]{:S(2)}, u32[]{:S(2)}) collective-permute-start(s32[2,8]{1,0:T(2,128)S(1)} %broadcast_select_fusion.16), channel_id=1, source_target_pairs={{256,0},{272,16},{288,32},{304,48},{320,64},{336,80},{352,96},{368... | collective-permute-start | bytes 200 | tf_op jit(solution)/shard_map/ppermute | solution.py:18
  104.0 4.8 %collective-permute-start.21 = (s32[2,8]{1,0:T(2,128)S(1)}, s32[2,8]{1,0:T(2,128)S(1)}, u32[]{:S(2)}, u32[]{:S(2)}) collective-permute-start(s32[2,8]{1,0:T(2,128)S(1)} %broadcast_select_fusion.15), channel_id=1, source_target_pairs={{256,0},{272,16},{288,32},{304,48},{320,64},{336,80},{352,96},{368... | collective-permute-start | bytes 200 | tf_op jit(solution)/shard_map/ppermute | solution.py:18
  110.9 3.8 collective-permute-start.23
  114.6 5.4 %collective-permute-done.9 = bf16[8,128,128]{2,1,0:T(8,128)(2,1)S(1)} collective-permute-done((bf16[8,128,128]{2,1,0:T(8,128)(2,1)S(1)}, bf16[8,128,128]{2,1,0:T(8,128)(2,1)S(1)}, u32[]{:S(2)}, u32[]{:S(2)}) %collective-permute-start.9) | collective-permute-done | bytes 262176 | tf_op jit(solution)/shard_map/ppermute | solution.py:18
  122.1 5.7 %collective-permute-start.31 = (s32[2,8]{1,0:T(2,128)S(1)}, s32[2,8]{1,0:T(2,128)S(1)}, u32[]{:S(2)}, u32[]{:S(2)}) collective-permute-start(s32[2,8]{1,0:T(2,128)S(1)} %get-tuple-element.7), channel_id=1, source_target_pairs={{32,0},{48,16},{64,32},{80,48},{96,64},{112,80},{128,96},{144,112}... | collective-permute-start | bytes 200 | tf_op jit(solution)/shard_map/ppermute | solution.py:18
  127.9 3.0 collective-permute-start.30
  130.9 3.1 collective-permute-done.30
  134.1 4.8 %collective-permute-start.37 = (s32[2,8]{1,0:T(2,128)S(1)}, s32[2,8]{1,0:T(2,128)S(1)}, u32[]{:S(2)}, u32[]{:S(2)}) collective-permute-start(s32[2,8]{1,0:T(2,128)S(1)} %collective-permute-done.31), channel_id=1, source_target_pairs={{32,0},{48,16},{64,32},{80,48},{96,64},{112,80},{128,96},{144,112}... | collective-permute-start | bytes 200 | tf_op jit(solution)/shard_map/ppermute | solution.py:18
  138.9 2.7 collective-permute-start.36
  141.7 5.4 %collective-permute-start.11 = (bf16[8,128,128]{2,1,0:T(8,128)(2,1)S(1)}, bf16[8,128,128]{2,1,0:T(8,128)(2,1)S(1)}, u32[]{:S(2)}, u32[]{:S(2)}) collective-permute-start(bf16[8,128,128]{2,1,0:T(8,128)(2,1)S(1)} %broadcast_select_fusion.7), channel_id=1, source_target_pairs={{8,0},{9,1},{10,2},{11,3},{12,4},{13,5},{14,6},{15,7},{0,8},{1,9},... | collective-permute-start | bytes 786440 | tf_op jit(solution)/shard_map/ppermute | solution.py:18
  147.2 2.3 collective-permute-start.24
  149.6 6.0 %collective-permute-start.43 = (s32[2,8]{1,0:T(2,128)S(1)}, s32[2,8]{1,0:T(2,128)S(1)}, u32[]{:S(2)}, u32[]{:S(2)}) collective-permute-start(s32[2,8]{1,0:T(2,128)S(1)} %collective-permute-done.37), channel_id=1, source_target_pairs={{32,0},{48,16},{64,32},{80,48},{96,64},{112,80},{128,96},{144,112}... | collective-permute-start | bytes 200 | tf_op jit(solution)/shard_map/ppermute | solution.py:18
  155.7 2.7 collective-permute-start.42
  158.4 3.1 collective-permute-done.42
  161.6 5.6 %collective-permute-start.29 = (bf16[8,128,128]{2,1,0:T(8,128)(2,1)S(1)}, bf16[8,128,128]{2,1,0:T(8,128)(2,1)S(1)}, u32[]{:S(2)}, u32[]{:S(2)}) collective-permute-start(bf16[8,128,128]{2,1,0:T(8,128)(2,1)S(1)} %broadcast_select_fusion.8), channel_id=1, source_target_pairs={{1,0},{2,1},{3,2},{4,3},{5,4},{6,5},{7,6},{8,7},{9,8},{10,9},{11,1... | collective-permute-start | bytes 786440 | tf_op jit(solution)/shard_map/ppermute | solution.py:18
  171.7 4.9 %collective-permute-done.35 = bf16[8,128,128]{2,1,0:T(8,128)(2,1)S(1)} collective-permute-done((bf16[8,128,128]{2,1,0:T(8,128)(2,1)S(1)}, bf16[8,128,128]{2,1,0:T(8,128)(2,1)S(1)}, u32[]{:S(2)}, u32[]{:S(2)}) %collective-permute-start.35) | collective-permute-done | bytes 262176 | tf_op jit(solution)/shard_map/ppermute | solution.py:18
  178.2 15.1 %collective-permute-done.25 = bf16[2,8,128,128]{3,2,1,0:T(8,128)(2,1)S(1)} collective-permute-done((bf16[2,8,128,128]{3,2,1,0:T(8,128)(2,1)S(1)}, bf16[2,8,128,128]{3,2,1,0:T(8,128)(2,1)S(1)}, u32[]{:S(2)}, u32[]{:S(2)}) %collective-permute-start.25) | collective-permute-done | bytes 524320 | tf_op jit(solution)/shard_map/ppermute | solution.py:18
  193.4 4.2 %collective-permute-start.26 = (bf16[2,8,128,128]{3,2,1,0:T(8,128)(2,1)S(1)}, bf16[2,8,128,128]{3,2,1,0:T(8,128)(2,1)S(1)}, u32[]{:S(2)}, u32[]{:S(2)}) collective-permute-start(bf16[2,8,128,128]{3,2,1,0:T(8,128)(2,1)S(1)} %broadcast_select_fusion.3), channel_id=1, source_target_pairs={{256,0},{272,16},{288,32},{304,48},{320,64},{336,80},{352,96},{368... | collective-permute-start | bytes 1572872 | tf_op jit(solution)/shard_map/ppermute | solution.py:18
  198.6 25.7 %collective-permute-done.26 = bf16[2,8,128,128]{3,2,1,0:T(8,128)(2,1)S(1)} collective-permute-done((bf16[2,8,128,128]{3,2,1,0:T(8,128)(2,1)S(1)}, bf16[2,8,128,128]{3,2,1,0:T(8,128)(2,1)S(1)}, u32[]{:S(2)}, u32[]{:S(2)}) %collective-permute-start.26) | collective-permute-done | bytes 524320 | tf_op jit(solution)/shard_map/ppermute | solution.py:18
  228.7 12.0 %collective-permute-done.32 = bf16[2,8,128,128]{3,2,1,0:T(8,128)(2,1)S(1)} collective-permute-done((bf16[2,8,128,128]{3,2,1,0:T(8,128)(2,1)S(1)}, bf16[2,8,128,128]{3,2,1,0:T(8,128)(2,1)S(1)}, u32[]{:S(2)}, u32[]{:S(2)}) %collective-permute-start.32) | collective-permute-done | bytes 524320 | tf_op jit(solution)/shard_map/ppermute | solution.py:18
  240.7 4.3 %collective-permute-start.38 = (bf16[2,8,128,128]{3,2,1,0:T(8,128)(2,1)S(1)}, bf16[2,8,128,128]{3,2,1,0:T(8,128)(2,1)S(1)}, u32[]{:S(2)}, u32[]{:S(2)}) collective-permute-start(bf16[2,8,128,128]{3,2,1,0:T(8,128)(2,1)S(1)} %collective-permute-done.32), channel_id=1, source_target_pairs={{32,0},{48,16},{64,32},{80,48},{96,64},{112,80},{128,96},{144,112}... | collective-permute-start | bytes 1572872 | tf_op jit(solution)/shard_map/ppermute | solution.py:18
  247.4 8.7 %collective-permute-done.38 = bf16[2,8,128,128]{3,2,1,0:T(8,128)(2,1)S(1)} collective-permute-done((bf16[2,8,128,128]{3,2,1,0:T(8,128)(2,1)S(1)}, bf16[2,8,128,128]{3,2,1,0:T(8,128)(2,1)S(1)}, u32[]{:S(2)}, u32[]{:S(2)}) %collective-permute-start.38) | collective-permute-done | bytes 524320 | tf_op jit(solution)/shard_map/ppermute | solution.py:18
  256.1 6.9 %collective-permute-start.44 = (bf16[2,8,128,128]{3,2,1,0:T(8,128)(2,1)S(1)}, bf16[2,8,128,128]{3,2,1,0:T(8,128)(2,1)S(1)}, u32[]{:S(2)}, u32[]{:S(2)}) collective-permute-start(bf16[2,8,128,128]{3,2,1,0:T(8,128)(2,1)S(1)} %collective-permute-done.38), channel_id=1, source_target_pairs={{32,0},{48,16},{64,32},{80,48},{96,64},{112,80},{128,96},{144,112}... | collective-permute-start | bytes 1572872 | tf_op jit(solution)/shard_map/ppermute | solution.py:18
  265.4 6.6 %collective-permute-done.44 = bf16[2,8,128,128]{3,2,1,0:T(8,128)(2,1)S(1)} collective-permute-done((bf16[2,8,128,128]{3,2,1,0:T(8,128)(2,1)S(1)}, bf16[2,8,128,128]{3,2,1,0:T(8,128)(2,1)S(1)}, u32[]{:S(2)}, u32[]{:S(2)}) %collective-permute-start.44) | collective-permute-done | bytes 524320 | tf_op jit(solution)/shard_map/ppermute | solution.py:18
  272.9 2.7 fusion.59
  277.0 101.6 %psum.7 = f32[]{:T(128)} all-reduce(f32[]{:T(128)S(6)} %select_n.252), channel_id=1, replica_groups=mesh['row'=32,'col'=16] {'row','col'}, use_global_device_ids=true, to_apply=%region_1.2 | all-reduce | flops 1 | bytes 8 | tf_op jit(solution)/shard_map/psum | solution.py:103
  (102 shorter events, 39.2 us)
Async XLA Ops:
  0.6 110.1 %copy-start = (bf16[1,1,2,8,128,128]{5,4,3,2,1,0:T(8,128)(2,1)S(1)}, bf16[1,1,2,8,128,128]{5,4,3,2,1,0:T(8,128)(2,1)}, u32[]{:S(2)}) copy-start(bf16[1,1,2,8,128,128]{5,4,3,2,1,0:T(8,128)(2,1)} %param.4) | copy-start | bytes 1572868
  0.6 29.2 %collective-permute-start.12 = (s32[2,8]{1,0:T(2,128)}, s32[2,8]{1,0:T(2,128)S(1)}, u32[]{:S(2)}, u32[]{:S(2)}) collective-permute-start(s32[2,8]{1,0:T(2,128)} %bitcast.239), channel_id=1, source_target_pairs={{496,0},{0,16},{16,32},{32,48},{48,64},{64,80},{80,96},{96,112},{1... | collective-permute-start | bytes 200 | tf_op jit(solution)/shard_map/ppermute | solution.py:18
  5.5 27.3 %collective-permute-start.17 = (s32[2,8]{1,0:T(2,128)S(1)}, s32[2,8]{1,0:T(2,128)S(1)}, u32[]{:S(2)}, u32[]{:S(2)}) collective-permute-start(s32[2,8]{1,0:T(2,128)S(1)} %bitcast_add_fusion), channel_id=1, source_target_pairs={{496,0},{0,16},{16,32},{32,48},{48,64},{64,80},{80,96},{96,112},{1... | collective-permute-start | bytes 200 | tf_op jit(solution)/shard_map/ppermute | solution.py:18
  10.5 100.3 %collective-permute-start.22 = (bf16[2,8,128,128]{3,2,1,0:T(8,128)(2,1)S(1)}, bf16[2,8,128,128]{3,2,1,0:T(8,128)(2,1)S(1)}, u32[]{:S(2)}, u32[]{:S(2)}) collective-permute-start(bf16[2,8,128,128]{3,2,1,0:T(8,128)(2,1)S(1)} %bitcast_multiply_fusion), channel_id=1, source_target_pairs={{496,0},{0,16},{16,32},{32,48},{48,64},{64,80},{80,96},{96,112},{1... | collective-permute-start | bytes 1572872 | tf_op jit(solution)/shard_map/ppermute | solution.py:18
  13.4 95.4 %collective-permute-start.8 = (bf16[8,128,128]{2,1,0:T(8,128)(2,1)S(1)}, bf16[8,128,128]{2,1,0:T(8,128)(2,1)S(1)}, u32[]{:S(2)}, u32[]{:S(2)}) collective-permute-start(bf16[8,128,128]{2,1,0:T(8,128)(2,1)S(1)} %dynamic-slice_bitcast_fusion), channel_id=1, source_target_pairs={{15,0},{0,1},{1,2},{2,3},{3,4},{4,5},{5,6},{6,7},{7,8},{8,9},{9,10... | collective-permute-start | bytes 786440 | tf_op jit(solution)/shard_map/ppermute | solution.py:18
  17.6 2.7 collective-permute-start
  20.2 7.0 %collective-permute-start.4 = (s32[8]{0:T(128)S(1)}, s32[8]{0:T(128)S(1)}, u32[]{:S(2)}, u32[]{:S(2)}) collective-permute-start(s32[8]{0:T(128)S(1)} %fusion.58), channel_id=1, source_target_pairs={{15,0},{0,1},{1,2},{2,3},{3,4},{4,5},{5,6},{6,7},{7,8},{8,9},{9,10... | collective-permute-start | bytes 104 | tf_op jit(solution)/shard_map/ppermute | solution.py:18
  27.3 11.0 %collective-permute-start.1 = (s32[8]{0:T(128)S(1)}, s32[8]{0:T(128)S(1)}, u32[]{:S(2)}, u32[]{:S(2)}) collective-permute-start(s32[8]{0:T(128)S(1)} %broadcast_select_fusion.20), channel_id=1, source_target_pairs={{14,0},{15,1},{0,2},{1,3},{2,4},{3,5},{4,6},{5,7},{6,8},{7,9},{8,1... | collective-permute-start | bytes 104 | tf_op jit(solution)/shard_map/ppermute | solution.py:18
  29.9 11.5 %collective-permute-start.5 = (s32[8]{0:T(128)S(1)}, s32[8]{0:T(128)S(1)}, u32[]{:S(2)}, u32[]{:S(2)}) collective-permute-start(s32[8]{0:T(128)S(1)} %broadcast_select_fusion.19), channel_id=1, source_target_pairs={{14,0},{15,1},{0,2},{1,3},{2,4},{3,5},{4,6},{5,7},{6,8},{7,9},{8,1... | collective-permute-start | bytes 104 | tf_op jit(solution)/shard_map/ppermute | solution.py:18
  32.8 29.3 %collective-permute-start.13 = (s32[2,8]{1,0:T(2,128)S(1)}, s32[2,8]{1,0:T(2,128)S(1)}, u32[]{:S(2)}, u32[]{:S(2)}) collective-permute-start(s32[2,8]{1,0:T(2,128)S(1)} %broadcast_select_fusion.10), channel_id=1, source_target_pairs={{480,0},{496,16},{0,32},{16,48},{32,64},{48,80},{64,96},{80,112},{... | collective-permute-start | bytes 200 | tf_op jit(solution)/shard_map/ppermute | solution.py:18
  38.2 25.8 %collective-permute-start.18 = (s32[2,8]{1,0:T(2,128)S(1)}, s32[2,8]{1,0:T(2,128)S(1)}, u32[]{:S(2)}, u32[]{:S(2)}) collective-permute-start(s32[2,8]{1,0:T(2,128)S(1)} %broadcast_select_fusion.9), channel_id=1, source_target_pairs={{480,0},{496,16},{0,32},{16,48},{32,64},{48,80},{64,96},{80,112},{... | collective-permute-start | bytes 200 | tf_op jit(solution)/shard_map/ppermute | solution.py:18
  41.4 6.9 %collective-permute-start.2 = (s32[8]{0:T(128)S(1)}, s32[8]{0:T(128)S(1)}, u32[]{:S(2)}, u32[]{:S(2)}) collective-permute-start(s32[8]{0:T(128)S(1)} %broadcast_select_fusion.22), channel_id=1, source_target_pairs={{12,0},{13,1},{14,2},{15,3},{0,4},{1,5},{2,6},{3,7},{4,8},{5,9},{6... | collective-permute-start | bytes 104 | tf_op jit(solution)/shard_map/ppermute | solution.py:18
  48.3 6.4 %collective-permute-start.6 = (s32[8]{0:T(128)S(1)}, s32[8]{0:T(128)S(1)}, u32[]{:S(2)}, u32[]{:S(2)}) collective-permute-start(s32[8]{0:T(128)S(1)} %broadcast_select_fusion.21), channel_id=1, source_target_pairs={{12,0},{13,1},{14,2},{15,3},{0,4},{1,5},{2,6},{3,7},{4,8},{5,9},{6... | collective-permute-start | bytes 104 | tf_op jit(solution)/shard_map/ppermute | solution.py:18
  54.7 12.7 %collective-permute-start.3 = (s32[8]{0:T(128)S(1)}, s32[8]{0:T(128)S(1)}, u32[]{:S(2)}, u32[]{:S(2)}) collective-permute-start(s32[8]{0:T(128)S(1)} %broadcast_select_fusion.24), channel_id=1, source_target_pairs={{8,0},{9,1},{10,2},{11,3},{12,4},{13,5},{14,6},{15,7},{0,8},{1,9},... | collective-permute-start | bytes 104 | tf_op jit(solution)/shard_map/ppermute | solution.py:18
  62.1 8.4 %collective-permute-start.7 = (s32[8]{0:T(128)S(1)}, s32[8]{0:T(128)S(1)}, u32[]{:S(2)}, u32[]{:S(2)}) collective-permute-start(s32[8]{0:T(128)S(1)} %broadcast_select_fusion.23), channel_id=1, source_target_pairs={{8,0},{9,1},{10,2},{11,3},{12,4},{13,5},{14,6},{15,7},{0,8},{1,9},... | collective-permute-start | bytes 104 | tf_op jit(solution)/shard_map/ppermute | solution.py:18
  64.1 19.6 %collective-permute-start.14 = (s32[2,8]{1,0:T(2,128)S(1)}, s32[2,8]{1,0:T(2,128)S(1)}, u32[]{:S(2)}, u32[]{:S(2)}) collective-permute-start(s32[2,8]{1,0:T(2,128)S(1)} %broadcast_select_fusion.12), channel_id=1, source_target_pairs={{448,0},{464,16},{480,32},{496,48},{0,64},{16,80},{32,96},{48,112}... | collective-permute-start | bytes 200 | tf_op jit(solution)/shard_map/ppermute | solution.py:18
  67.3 19.2 %collective-permute-start.19 = (s32[2,8]{1,0:T(2,128)S(1)}, s32[2,8]{1,0:T(2,128)S(1)}, u32[]{:S(2)}, u32[]{:S(2)}) collective-permute-start(s32[2,8]{1,0:T(2,128)S(1)} %broadcast_select_fusion.11), channel_id=1, source_target_pairs={{448,0},{464,16},{480,32},{496,48},{0,64},{16,80},{32,96},{48,112}... | collective-permute-start | bytes 200 | tf_op jit(solution)/shard_map/ppermute | solution.py:18
  70.6 8.4 %collective-permute-start.28 = (s32[8]{0:T(128)S(1)}, s32[8]{0:T(128)S(1)}, u32[]{:S(2)}, u32[]{:S(2)}) collective-permute-start(s32[8]{0:T(128)S(1)} %get-tuple-element.4), channel_id=1, source_target_pairs={{1,0},{2,1},{3,2},{4,3},{5,4},{6,5},{7,6},{8,7},{9,8},{10,9},{11,1... | collective-permute-start | bytes 104 | tf_op jit(solution)/shard_map/ppermute | solution.py:18
  79.0 3.0 collective-permute-start.27
  82.0 9.1 %collective-permute-start.34 = (s32[8]{0:T(128)S(1)}, s32[8]{0:T(128)S(1)}, u32[]{:S(2)}, u32[]{:S(2)}) collective-permute-start(s32[8]{0:T(128)S(1)} %collective-permute-done.28), channel_id=1, source_target_pairs={{1,0},{2,1},{3,2},{4,3},{5,4},{6,5},{7,6},{8,7},{9,8},{10,9},{11,1... | collective-permute-start | bytes 104 | tf_op jit(solution)/shard_map/ppermute | solution.py:18
  83.7 9.9 %collective-permute-start.33 = (s32[8]{0:T(128)S(1)}, s32[8]{0:T(128)S(1)}, u32[]{:S(2)}, u32[]{:S(2)}) collective-permute-start(s32[8]{0:T(128)S(1)} %collective-permute-done.27), channel_id=1, source_target_pairs={{1,0},{2,1},{3,2},{4,3},{5,4},{6,5},{7,6},{8,7},{9,8},{10,9},{11,1... | collective-permute-start | bytes 104 | tf_op jit(solution)/shard_map/ppermute | solution.py:18
  86.6 13.0 %collective-permute-start.15 = (s32[2,8]{1,0:T(2,128)S(1)}, s32[2,8]{1,0:T(2,128)S(1)}, u32[]{:S(2)}, u32[]{:S(2)}) collective-permute-start(s32[2,8]{1,0:T(2,128)S(1)} %broadcast_select_fusion.14), channel_id=1, source_target_pairs={{384,0},{400,16},{416,32},{432,48},{448,64},{464,80},{480,96},{496... | collective-permute-start | bytes 200 | tf_op jit(solution)/shard_map/ppermute | solution.py:18
  91.1 12.8 %collective-permute-start.20 = (s32[2,8]{1,0:T(2,128)S(1)}, s32[2,8]{1,0:T(2,128)S(1)}, u32[]{:S(2)}, u32[]{:S(2)}) collective-permute-start(s32[2,8]{1,0:T(2,128)S(1)} %broadcast_select_fusion.13), channel_id=1, source_target_pairs={{384,0},{400,16},{416,32},{432,48},{448,64},{464,80},{480,96},{496... | collective-permute-start | bytes 200 | tf_op jit(solution)/shard_map/ppermute | solution.py:18
  93.6 3.0 collective-permute-start.40
  96.5 3.0 collective-permute-start.39
  99.5 22.5 %collective-permute-start.16 = (s32[2,8]{1,0:T(2,128)S(1)}, s32[2,8]{1,0:T(2,128)S(1)}, u32[]{:S(2)}, u32[]{:S(2)}) collective-permute-start(s32[2,8]{1,0:T(2,128)S(1)} %broadcast_select_fusion.16), channel_id=1, source_target_pairs={{256,0},{272,16},{288,32},{304,48},{320,64},{336,80},{352,96},{368... | collective-permute-start | bytes 200 | tf_op jit(solution)/shard_map/ppermute | solution.py:18
  104.0 18.1 %collective-permute-start.21 = (s32[2,8]{1,0:T(2,128)S(1)}, s32[2,8]{1,0:T(2,128)S(1)}, u32[]{:S(2)}, u32[]{:S(2)}) collective-permute-start(s32[2,8]{1,0:T(2,128)S(1)} %broadcast_select_fusion.15), channel_id=1, source_target_pairs={{256,0},{272,16},{288,32},{304,48},{320,64},{336,80},{352,96},{368... | collective-permute-start | bytes 200 | tf_op jit(solution)/shard_map/ppermute | solution.py:18
  108.8 11.2 %collective-permute-start.9 = (bf16[8,128,128]{2,1,0:T(8,128)(2,1)S(1)}, bf16[8,128,128]{2,1,0:T(8,128)(2,1)S(1)}, u32[]{:S(2)}, u32[]{:S(2)}) collective-permute-start(bf16[8,128,128]{2,1,0:T(8,128)(2,1)S(1)} %broadcast_select_fusion.5), channel_id=1, source_target_pairs={{14,0},{15,1},{0,2},{1,3},{2,4},{3,5},{4,6},{5,7},{6,8},{7,9},{8,1... | collective-permute-start | bytes 786440 | tf_op jit(solution)/shard_map/ppermute | solution.py:18
  110.9 36.3 %collective-permute-start.23 = (bf16[2,8,128,128]{3,2,1,0:T(8,128)(2,1)S(1)}, bf16[2,8,128,128]{3,2,1,0:T(8,128)(2,1)S(1)}, u32[]{:S(2)}, u32[]{:S(2)}) collective-permute-start(bf16[2,8,128,128]{3,2,1,0:T(8,128)(2,1)S(1)} %broadcast_select_fusion), channel_id=1, source_target_pairs={{480,0},{496,16},{0,32},{16,48},{32,64},{48,80},{64,96},{80,112},{... | collective-permute-start | bytes 1572872 | tf_op jit(solution)/shard_map/ppermute | solution.py:18
  120.1 21.6 %collective-permute-start.10 = (bf16[8,128,128]{2,1,0:T(8,128)(2,1)S(1)}, bf16[8,128,128]{2,1,0:T(8,128)(2,1)S(1)}, u32[]{:S(2)}, u32[]{:S(2)}) collective-permute-start(bf16[8,128,128]{2,1,0:T(8,128)(2,1)S(1)} %broadcast_select_fusion.6), channel_id=1, source_target_pairs={{12,0},{13,1},{14,2},{15,3},{0,4},{1,5},{2,6},{3,7},{4,8},{5,9},{6... | collective-permute-start | bytes 786440 | tf_op jit(solution)/shard_map/ppermute | solution.py:18
  122.1 8.8 %collective-permute-start.31 = (s32[2,8]{1,0:T(2,128)S(1)}, s32[2,8]{1,0:T(2,128)S(1)}, u32[]{:S(2)}, u32[]{:S(2)}) collective-permute-start(s32[2,8]{1,0:T(2,128)S(1)} %get-tuple-element.7), channel_id=1, source_target_pairs={{32,0},{48,16},{64,32},{80,48},{96,64},{112,80},{128,96},{144,112}... | collective-permute-start | bytes 200 | tf_op jit(solution)/shard_map/ppermute | solution.py:18
  127.9 6.1 %collective-permute-start.30 = (s32[2,8]{1,0:T(2,128)S(1)}, s32[2,8]{1,0:T(2,128)S(1)}, u32[]{:S(2)}, u32[]{:S(2)}) collective-permute-start(s32[2,8]{1,0:T(2,128)S(1)} %get-tuple-element.6), channel_id=1, source_target_pairs={{32,0},{48,16},{64,32},{80,48},{96,64},{112,80},{128,96},{144,112}... | collective-permute-start | bytes 200 | tf_op jit(solution)/shard_map/ppermute | solution.py:18
  134.1 15.5 %collective-permute-start.37 = (s32[2,8]{1,0:T(2,128)S(1)}, s32[2,8]{1,0:T(2,128)S(1)}, u32[]{:S(2)}, u32[]{:S(2)}) collective-permute-start(s32[2,8]{1,0:T(2,128)S(1)} %collective-permute-done.31), channel_id=1, source_target_pairs={{32,0},{48,16},{64,32},{80,48},{96,64},{112,80},{128,96},{144,112}... | collective-permute-start | bytes 200 | tf_op jit(solution)/shard_map/ppermute | solution.py:18
  138.9 10.6 %collective-permute-start.36 = (s32[2,8]{1,0:T(2,128)S(1)}, s32[2,8]{1,0:T(2,128)S(1)}, u32[]{:S(2)}, u32[]{:S(2)}) collective-permute-start(s32[2,8]{1,0:T(2,128)S(1)} %collective-permute-done.30), channel_id=1, source_target_pairs={{32,0},{48,16},{64,32},{80,48},{96,64},{112,80},{128,96},{144,112}... | collective-permute-start | bytes 200 | tf_op jit(solution)/shard_map/ppermute | solution.py:18
  141.7 19.9 %collective-permute-start.11 = (bf16[8,128,128]{2,1,0:T(8,128)(2,1)S(1)}, bf16[8,128,128]{2,1,0:T(8,128)(2,1)S(1)}, u32[]{:S(2)}, u32[]{:S(2)}) collective-permute-start(bf16[8,128,128]{2,1,0:T(8,128)(2,1)S(1)} %broadcast_select_fusion.7), channel_id=1, source_target_pairs={{8,0},{9,1},{10,2},{11,3},{12,4},{13,5},{14,6},{15,7},{0,8},{1,9},... | collective-permute-start | bytes 786440 | tf_op jit(solution)/shard_map/ppermute | solution.py:18
  147.2 20.0 %collective-permute-start.24 = (bf16[2,8,128,128]{3,2,1,0:T(8,128)(2,1)S(1)}, bf16[2,8,128,128]{3,2,1,0:T(8,128)(2,1)S(1)}, u32[]{:S(2)}, u32[]{:S(2)}) collective-permute-start(bf16[2,8,128,128]{3,2,1,0:T(8,128)(2,1)S(1)} %broadcast_select_fusion.1), channel_id=1, source_target_pairs={{448,0},{464,16},{480,32},{496,48},{0,64},{16,80},{32,96},{48,112}... | collective-permute-start | bytes 1572872 | tf_op jit(solution)/shard_map/ppermute | solution.py:18
  149.6 8.8 %collective-permute-start.43 = (s32[2,8]{1,0:T(2,128)S(1)}, s32[2,8]{1,0:T(2,128)S(1)}, u32[]{:S(2)}, u32[]{:S(2)}) collective-permute-start(s32[2,8]{1,0:T(2,128)S(1)} %collective-permute-done.37), channel_id=1, source_target_pairs={{32,0},{48,16},{64,32},{80,48},{96,64},{112,80},{128,96},{144,112}... | collective-permute-start | bytes 200 | tf_op jit(solution)/shard_map/ppermute | solution.py:18
  155.7 5.8 %collective-permute-start.42 = (s32[2,8]{1,0:T(2,128)S(1)}, s32[2,8]{1,0:T(2,128)S(1)}, u32[]{:S(2)}, u32[]{:S(2)}) collective-permute-start(s32[2,8]{1,0:T(2,128)S(1)} %collective-permute-done.36), channel_id=1, source_target_pairs={{32,0},{48,16},{64,32},{80,48},{96,64},{112,80},{128,96},{144,112}... | collective-permute-start | bytes 200 | tf_op jit(solution)/shard_map/ppermute | solution.py:18
  161.6 8.8 %collective-permute-start.29 = (bf16[8,128,128]{2,1,0:T(8,128)(2,1)S(1)}, bf16[8,128,128]{2,1,0:T(8,128)(2,1)S(1)}, u32[]{:S(2)}, u32[]{:S(2)}) collective-permute-start(bf16[8,128,128]{2,1,0:T(8,128)(2,1)S(1)} %broadcast_select_fusion.8), channel_id=1, source_target_pairs={{1,0},{2,1},{3,2},{4,3},{5,4},{6,5},{7,6},{8,7},{9,8},{10,9},{11,1... | collective-permute-start | bytes 786440 | tf_op jit(solution)/shard_map/ppermute | solution.py:18
  167.3 26.0 %collective-permute-start.25 = (bf16[2,8,128,128]{3,2,1,0:T(8,128)(2,1)S(1)}, bf16[2,8,128,128]{3,2,1,0:T(8,128)(2,1)S(1)}, u32[]{:S(2)}, u32[]{:S(2)}) collective-permute-start(bf16[2,8,128,128]{3,2,1,0:T(8,128)(2,1)S(1)} %broadcast_select_fusion.2), channel_id=1, source_target_pairs={{384,0},{400,16},{416,32},{432,48},{448,64},{464,80},{480,96},{496... | collective-permute-start | bytes 1572872 | tf_op jit(solution)/shard_map/ppermute | solution.py:18
  170.5 6.1 %collective-permute-start.35 = (bf16[8,128,128]{2,1,0:T(8,128)(2,1)S(1)}, bf16[8,128,128]{2,1,0:T(8,128)(2,1)S(1)}, u32[]{:S(2)}, u32[]{:S(2)}) collective-permute-start(bf16[8,128,128]{2,1,0:T(8,128)(2,1)S(1)} %collective-permute-done.29), channel_id=1, source_target_pairs={{1,0},{2,1},{3,2},{4,3},{5,4},{6,5},{7,6},{8,7},{9,8},{10,9},{11,1... | collective-permute-start | bytes 786440 | tf_op jit(solution)/shard_map/ppermute | solution.py:18
  176.6 21.5 %collective-permute-start.41 = (bf16[8,128,128]{2,1,0:T(8,128)(2,1)S(1)}, bf16[8,128,128]{2,1,0:T(8,128)(2,1)S(1)}, u32[]{:S(2)}, u32[]{:S(2)}) collective-permute-start(bf16[8,128,128]{2,1,0:T(8,128)(2,1)S(1)} %collective-permute-done.35), channel_id=1, source_target_pairs={{1,0},{2,1},{3,2},{4,3},{5,4},{6,5},{7,6},{8,7},{9,8},{10,9},{11,1... | collective-permute-start | bytes 786440 | tf_op jit(solution)/shard_map/ppermute | solution.py:18
  193.4 30.9 %collective-permute-start.26 = (bf16[2,8,128,128]{3,2,1,0:T(8,128)(2,1)S(1)}, bf16[2,8,128,128]{3,2,1,0:T(8,128)(2,1)S(1)}, u32[]{:S(2)}, u32[]{:S(2)}) collective-permute-start(bf16[2,8,128,128]{3,2,1,0:T(8,128)(2,1)S(1)} %broadcast_select_fusion.3), channel_id=1, source_target_pairs={{256,0},{272,16},{288,32},{304,48},{320,64},{336,80},{352,96},{368... | collective-permute-start | bytes 1572872 | tf_op jit(solution)/shard_map/ppermute | solution.py:18
  224.3 16.3 %collective-permute-start.32 = (bf16[2,8,128,128]{3,2,1,0:T(8,128)(2,1)S(1)}, bf16[2,8,128,128]{3,2,1,0:T(8,128)(2,1)S(1)}, u32[]{:S(2)}, u32[]{:S(2)}) collective-permute-start(bf16[2,8,128,128]{3,2,1,0:T(8,128)(2,1)S(1)} %broadcast_select_fusion.4), channel_id=1, source_target_pairs={{32,0},{48,16},{64,32},{80,48},{96,64},{112,80},{128,96},{144,112}... | collective-permute-start | bytes 1572872 | tf_op jit(solution)/shard_map/ppermute | solution.py:18
  240.7 15.4 %collective-permute-start.38 = (bf16[2,8,128,128]{3,2,1,0:T(8,128)(2,1)S(1)}, bf16[2,8,128,128]{3,2,1,0:T(8,128)(2,1)S(1)}, u32[]{:S(2)}, u32[]{:S(2)}) collective-permute-start(bf16[2,8,128,128]{3,2,1,0:T(8,128)(2,1)S(1)} %collective-permute-done.32), channel_id=1, source_target_pairs={{32,0},{48,16},{64,32},{80,48},{96,64},{112,80},{128,96},{144,112}... | collective-permute-start | bytes 1572872 | tf_op jit(solution)/shard_map/ppermute | solution.py:18
  256.1 16.0 %collective-permute-start.44 = (bf16[2,8,128,128]{3,2,1,0:T(8,128)(2,1)S(1)}, bf16[2,8,128,128]{3,2,1,0:T(8,128)(2,1)S(1)}, u32[]{:S(2)}, u32[]{:S(2)}) collective-permute-start(bf16[2,8,128,128]{3,2,1,0:T(8,128)(2,1)S(1)} %collective-permute-done.38), channel_id=1, source_target_pairs={{32,0},{48,16},{64,32},{80,48},{96,64},{112,80},{128,96},{144,112}... | collective-permute-start | bytes 1572872 | tf_op jit(solution)/shard_map/ppermute | solution.py:18
where the time goes:
time: 382 us; the launch traced here: 380 us
  starting transfers between devices  151 us (40%)
  waiting for transfers between devices  102 us (27%)
  blocking collectives  102 us (27%)
  matrix products  12.7 us (3%)
  other arithmetic  6.7 us (2%)
  between operations  3.84 us (1%)
    ppermute x45, starting transfers between devices, passed_along(): return lax.ppermute(block, axis, route)  151 us
    ppermute x45, waiting for transfers between devices, passed_along(): return lax.ppermute(block, axis, route)  102 us
    psum x1, blocking collectives, body(): overall = lax.psum(term, ('row', 'col'))  102 us
  transfers between devices with their start and end apart: 45, of which 18 were waited for; matrix products, arithmetic and copies ran while one was open for 4% of the time, Pallas kernels for 0%

commit v1 on v0

--- a/solution.py
+++ b/solution.py
@@ -100,7 +100,7 @@
     start = jnp.clip(shift_amount, 0, groups - 1) * RB * width
     window = lax.dynamic_slice_in_dim(totals, start, RB * width, 1)
     term = jnp.where(valid, jnp.trace(window), jnp.zeros((), jnp.float32))
-    overall = lax.psum(term, ("row", "col"))
+    overall = lax.psum(lax.psum(term, "row"), "col")
     trace_value = overall / math.sqrt(row_count * RB * width)
     return (totals.astype(jnp.bfloat16), trace_value)
 

time: 382 us -> 383 us (level)
    psum x1 -> x2, blocking collectives: 102 us -> 103 us  [body(): overall = lax.psum(lax.psum(term, 'row'), 'col')]
where the time goes in v1:
time: 383 us; the launch traced here: 382 us
  starting transfers between devices  151 us (39%)
  blocking collectives  103 us (27%)
  waiting for transfers between devices  102 us (27%)
  matrix products  12.7 us (3%)
  other arithmetic  6.7 us (2%)
  between operations  3.84 us (1%)
    ppermute x45, starting transfers between devices, passed_along(): return lax.ppermute(block, axis, route)  151 us
    psum x2, blocking collectives, body(): overall = lax.psum(lax.psum(term, 'row'), 'col')  103 us
    ppermute x45, waiting for transfers between devices, passed_along(): return lax.ppermute(block, axis, route)  102 us
  transfers between devices with their start and end apart: 45, of which 18 were waited for; matrix products, arithmetic and copies ran while one was open for 4% of the time, Pallas kernels for 0%

profile of v1, /device:TPU:1, one launch (start us, length us, event | category | flops | bytes accessed | tf_op | source)
XLA Modules:
  0.0 382.1 jit_solution(10839844568424554019)
XLA Ops:
  0.6 4.1 %collective-permute-start.12 = (s32[2,8]{1,0:T(2,128)}, s32[2,8]{1,0:T(2,128)S(1)}, u32[]{:S(2)}, u32[]{:S(2)}) collective-permute-start(s32[2,8]{1,0:T(2,128)} %bitcast.239), channel_id=1, source_target_pairs={{496,0},{0,16},{16,32},{32,48},{48,64},{64,80},{80,96},{96,112},{1... | collective-permute-start | bytes 200 | tf_op jit(solution)/shard_map/ppermute | solution.py:18
  5.5 3.1 collective-permute-start.17
  10.5 2.8 collective-permute-start.22
  13.4 3.5 collective-permute-start.8
  20.2 2.5 collective-permute-start.4
  23.4 3.9 %collective-permute-done.4 = s32[8]{0:T(128)S(1)} collective-permute-done((s32[8]{0:T(128)S(1)}, s32[8]{0:T(128)S(1)}, u32[]{:S(2)}, u32[]{:S(2)}) %collective-permute-start.4) | collective-permute-done | bytes 64 | tf_op jit(solution)/shard_map/ppermute | solution.py:18
  29.9 2.3 collective-permute-start.5
  32.8 4.6 %collective-permute-start.13 = (s32[2,8]{1,0:T(2,128)S(1)}, s32[2,8]{1,0:T(2,128)S(1)}, u32[]{:S(2)}, u32[]{:S(2)}) collective-permute-start(s32[2,8]{1,0:T(2,128)S(1)} %broadcast_select_fusion.10), channel_id=1, source_target_pairs={{480,0},{496,16},{0,32},{16,48},{32,64},{48,80},{64,96},{80,112},{... | collective-permute-start | bytes 200 | tf_op jit(solution)/shard_map/ppermute | solution.py:18
  38.2 3.1 collective-permute-start.18
  41.4 6.2 %collective-permute-start.2 = (s32[8]{0:T(128)S(1)}, s32[8]{0:T(128)S(1)}, u32[]{:S(2)}, u32[]{:S(2)}) collective-permute-start(s32[8]{0:T(128)S(1)} %broadcast_select_fusion.22), channel_id=1, source_target_pairs={{12,0},{13,1},{14,2},{15,3},{0,4},{1,5},{2,6},{3,7},{4,8},{5,9},{6... | collective-permute-start | bytes 104 | tf_op jit(solution)/shard_map/ppermute | solution.py:18
  48.3 4.5 %collective-permute-start.6 = (s32[8]{0:T(128)S(1)}, s32[8]{0:T(128)S(1)}, u32[]{:S(2)}, u32[]{:S(2)}) collective-permute-start(s32[8]{0:T(128)S(1)} %broadcast_select_fusion.21), channel_id=1, source_target_pairs={{12,0},{13,1},{14,2},{15,3},{0,4},{1,5},{2,6},{3,7},{4,8},{5,9},{6... | collective-permute-start | bytes 104 | tf_op jit(solution)/shard_map/ppermute | solution.py:18
  54.7 7.5 %collective-permute-start.3 = (s32[8]{0:T(128)S(1)}, s32[8]{0:T(128)S(1)}, u32[]{:S(2)}, u32[]{:S(2)}) collective-permute-start(s32[8]{0:T(128)S(1)} %broadcast_select_fusion.24), channel_id=1, source_target_pairs={{8,0},{9,1},{10,2},{11,3},{12,4},{13,5},{14,6},{15,7},{0,8},{1,9},... | collective-permute-start | bytes 104 | tf_op jit(solution)/shard_map/ppermute | solution.py:18
  64.1 3.2 collective-permute-start.14
  67.3 3.2 collective-permute-start.19
  70.6 7.6 %collective-permute-start.28 = (s32[8]{0:T(128)S(1)}, s32[8]{0:T(128)S(1)}, u32[]{:S(2)}, u32[]{:S(2)}) collective-permute-start(s32[8]{0:T(128)S(1)} %get-tuple-element.4), channel_id=1, source_target_pairs={{1,0},{2,1},{3,2},{4,3},{5,4},{6,5},{7,6},{8,7},{9,8},{10,9},{11,1... | collective-permute-start | bytes 104 | tf_op jit(solution)/shard_map/ppermute | solution.py:18
  79.5 2.5 collective-permute-done.27
  83.7 2.9 collective-permute-start.33
  86.6 4.5 %collective-permute-start.15 = (s32[2,8]{1,0:T(2,128)S(1)}, s32[2,8]{1,0:T(2,128)S(1)}, u32[]{:S(2)}, u32[]{:S(2)}) collective-permute-start(s32[2,8]{1,0:T(2,128)S(1)} %broadcast_select_fusion.14), channel_id=1, source_target_pairs={{384,0},{400,16},{416,32},{432,48},{448,64},{464,80},{480,96},{496... | collective-permute-start | bytes 200 | tf_op jit(solution)/shard_map/ppermute | solution.py:18
  91.1 2.4 collective-permute-start.20
  94.2 2.4 collective-permute-done.40
  96.6 3.0 collective-permute-done.39
  99.5 4.4 %collective-permute-start.16 = (s32[2,8]{1,0:T(2,128)S(1)}, s32[2,8]{1,0:T(2,128)S(1)}, u32[]{:S(2)}, u32[]{:S(2)}) collective-permute-start(s32[2,8]{1,0:T(2,128)S(1)} %broadcast_select_fusion.16), channel_id=1, source_target_pairs={{256,0},{272,16},{288,32},{304,48},{320,64},{336,80},{352,96},{368... | collective-permute-start | bytes 200 | tf_op jit(solution)/shard_map/ppermute | solution.py:18
  104.0 4.8 %collective-permute-start.21 = (s32[2,8]{1,0:T(2,128)S(1)}, s32[2,8]{1,0:T(2,128)S(1)}, u32[]{:S(2)}, u32[]{:S(2)}) collective-permute-start(s32[2,8]{1,0:T(2,128)S(1)} %broadcast_select_fusion.15), channel_id=1, source_target_pairs={{256,0},{272,16},{288,32},{304,48},{320,64},{336,80},{352,96},{368... | collective-permute-start | bytes 200 | tf_op jit(solution)/shard_map/ppermute | solution.py:18
  110.9 3.8 collective-permute-start.23
  114.6 5.4 %collective-permute-done.9 = bf16[8,128,128]{2,1,0:T(8,128)(2,1)S(1)} collective-permute-done((bf16[8,128,128]{2,1,0:T(8,128)(2,1)S(1)}, bf16[8,128,128]{2,1,0:T(8,128)(2,1)S(1)}, u32[]{:S(2)}, u32[]{:S(2)}) %collective-permute-start.9) | collective-permute-done | bytes 262176 | tf_op jit(solution)/shard_map/ppermute | solution.py:18
  122.1 5.7 %collective-permute-start.31 = (s32[2,8]{1,0:T(2,128)S(1)}, s32[2,8]{1,0:T(2,128)S(1)}, u32[]{:S(2)}, u32[]{:S(2)}) collective-permute-start(s32[2,8]{1,0:T(2,128)S(1)} %get-tuple-element.7), channel_id=1, source_target_pairs={{32,0},{48,16},{64,32},{80,48},{96,64},{112,80},{128,96},{144,112}... | collective-permute-start | bytes 200 | tf_op jit(solution)/shard_map/ppermute | solution.py:18
  127.9 3.0 collective-permute-start.30
  130.9 3.1 collective-permute-done.30
  134.1 4.8 %collective-permute-start.37 = (s32[2,8]{1,0:T(2,128)S(1)}, s32[2,8]{1,0:T(2,128)S(1)}, u32[]{:S(2)}, u32[]{:S(2)}) collective-permute-start(s32[2,8]{1,0:T(2,128)S(1)} %collective-permute-done.31), channel_id=1, source_target_pairs={{32,0},{48,16},{64,32},{80,48},{96,64},{112,80},{128,96},{144,112}... | collective-permute-start | bytes 200 | tf_op jit(solution)/shard_map/ppermute | solution.py:18
  138.9 2.7 collective-permute-start.36
  141.7 5.4 %collective-permute-start.11 = (bf16[8,128,128]{2,1,0:T(8,128)(2,1)S(1)}, bf16[8,128,128]{2,1,0:T(8,128)(2,1)S(1)}, u32[]{:S(2)}, u32[]{:S(2)}) collective-permute-start(bf16[8,128,128]{2,1,0:T(8,128)(2,1)S(1)} %broadcast_select_fusion.7), channel_id=1, source_target_pairs={{8,0},{9,1},{10,2},{11,3},{12,4},{13,5},{14,6},{15,7},{0,8},{1,9},... | collective-permute-start | bytes 786440 | tf_op jit(solution)/shard_map/ppermute | solution.py:18
  147.2 2.3 collective-permute-start.24
  149.6 6.0 %collective-permute-start.43 = (s32[2,8]{1,0:T(2,128)S(1)}, s32[2,8]{1,0:T(2,128)S(1)}, u32[]{:S(2)}, u32[]{:S(2)}) collective-permute-start(s32[2,8]{1,0:T(2,128)S(1)} %collective-permute-done.37), channel_id=1, source_target_pairs={{32,0},{48,16},{64,32},{80,48},{96,64},{112,80},{128,96},{144,112}... | collective-permute-start | bytes 200 | tf_op jit(solution)/shard_map/ppermute | solution.py:18
  155.7 2.7 collective-permute-start.42
  158.4 3.1 collective-permute-done.42
  161.6 5.6 %collective-permute-start.29 = (bf16[8,128,128]{2,1,0:T(8,128)(2,1)S(1)}, bf16[8,128,128]{2,1,0:T(8,128)(2,1)S(1)}, u32[]{:S(2)}, u32[]{:S(2)}) collective-permute-start(bf16[8,128,128]{2,1,0:T(8,128)(2,1)S(1)} %broadcast_select_fusion.8), channel_id=1, source_target_pairs={{1,0},{2,1},{3,2},{4,3},{5,4},{6,5},{7,6},{8,7},{9,8},{10,9},{11,1... | collective-permute-start | bytes 786440 | tf_op jit(solution)/shard_map/ppermute | solution.py:18
  171.7 4.9 %collective-permute-done.35 = bf16[8,128,128]{2,1,0:T(8,128)(2,1)S(1)} collective-permute-done((bf16[8,128,128]{2,1,0:T(8,128)(2,1)S(1)}, bf16[8,128,128]{2,1,0:T(8,128)(2,1)S(1)}, u32[]{:S(2)}, u32[]{:S(2)}) %collective-permute-start.35) | collective-permute-done | bytes 262176 | tf_op jit(solution)/shard_map/ppermute | solution.py:18
  178.2 15.1 %collective-permute-done.25 = bf16[2,8,128,128]{3,2,1,0:T(8,128)(2,1)S(1)} collective-permute-done((bf16[2,8,128,128]{3,2,1,0:T(8,128)(2,1)S(1)}, bf16[2,8,128,128]{3,2,1,0:T(8,128)(2,1)S(1)}, u32[]{:S(2)}, u32[]{:S(2)}) %collective-permute-start.25) | collective-permute-done | bytes 524320 | tf_op jit(solution)/shard_map/ppermute | solution.py:18
  193.4 4.2 %collective-permute-start.26 = (bf16[2,8,128,128]{3,2,1,0:T(8,128)(2,1)S(1)}, bf16[2,8,128,128]{3,2,1,0:T(8,128)(2,1)S(1)}, u32[]{:S(2)}, u32[]{:S(2)}) collective-permute-start(bf16[2,8,128,128]{3,2,1,0:T(8,128)(2,1)S(1)} %broadcast_select_fusion.3), channel_id=1, source_target_pairs={{256,0},{272,16},{288,32},{304,48},{320,64},{336,80},{352,96},{368... | collective-permute-start | bytes 1572872 | tf_op jit(solution)/shard_map/ppermute | solution.py:18
  198.6 25.7 %collective-permute-done.26 = bf16[2,8,128,128]{3,2,1,0:T(8,128)(2,1)S(1)} collective-permute-done((bf16[2,8,128,128]{3,2,1,0:T(8,128)(2,1)S(1)}, bf16[2,8,128,128]{3,2,1,0:T(8,128)(2,1)S(1)}, u32[]{:S(2)}, u32[]{:S(2)}) %collective-permute-start.26) | collective-permute-done | bytes 524320 | tf_op jit(solution)/shard_map/ppermute | solution.py:18
  228.7 12.0 %collective-permute-done.32 = bf16[2,8,128,128]{3,2,1,0:T(8,128)(2,1)S(1)} collective-permute-done((bf16[2,8,128,128]{3,2,1,0:T(8,128)(2,1)S(1)}, bf16[2,8,128,128]{3,2,1,0:T(8,128)(2,1)S(1)}, u32[]{:S(2)}, u32[]{:S(2)}) %collective-permute-start.32) | collective-permute-done | bytes 524320 | tf_op jit(solution)/shard_map/ppermute | solution.py:18
  240.7 4.3 %collective-permute-start.38 = (bf16[2,8,128,128]{3,2,1,0:T(8,128)(2,1)S(1)}, bf16[2,8,128,128]{3,2,1,0:T(8,128)(2,1)S(1)}, u32[]{:S(2)}, u32[]{:S(2)}) collective-permute-start(bf16[2,8,128,128]{3,2,1,0:T(8,128)(2,1)S(1)} %collective-permute-done.32), channel_id=1, source_target_pairs={{32,0},{48,16},{64,32},{80,48},{96,64},{112,80},{128,96},{144,112}... | collective-permute-start | bytes 1572872 | tf_op jit(solution)/shard_map/ppermute | solution.py:18
  247.4 8.7 %collective-permute-done.38 = bf16[2,8,128,128]{3,2,1,0:T(8,128)(2,1)S(1)} collective-permute-done((bf16[2,8,128,128]{3,2,1,0:T(8,128)(2,1)S(1)}, bf16[2,8,128,128]{3,2,1,0:T(8,128)(2,1)S(1)}, u32[]{:S(2)}, u32[]{:S(2)}) %collective-permute-start.38) | collective-permute-done | bytes 524320 | tf_op jit(solution)/shard_map/ppermute | solution.py:18
  256.1 6.9 %collective-permute-start.44 = (bf16[2,8,128,128]{3,2,1,0:T(8,128)(2,1)S(1)}, bf16[2,8,128,128]{3,2,1,0:T(8,128)(2,1)S(1)}, u32[]{:S(2)}, u32[]{:S(2)}) collective-permute-start(bf16[2,8,128,128]{3,2,1,0:T(8,128)(2,1)S(1)} %collective-permute-done.38), channel_id=1, source_target_pairs={{32,0},{48,16},{64,32},{80,48},{96,64},{112,80},{128,96},{144,112}... | collective-permute-start | bytes 1572872 | tf_op jit(solution)/shard_map/ppermute | solution.py:18
  265.4 6.6 %collective-permute-done.44 = bf16[2,8,128,128]{3,2,1,0:T(8,128)(2,1)S(1)} collective-permute-done((bf16[2,8,128,128]{3,2,1,0:T(8,128)(2,1)S(1)}, bf16[2,8,128,128]{3,2,1,0:T(8,128)(2,1)S(1)}, u32[]{:S(2)}, u32[]{:S(2)}) %collective-permute-start.44) | collective-permute-done | bytes 524320 | tf_op jit(solution)/shard_map/ppermute | solution.py:18
  272.9 2.7 fusion.59
  277.0 63.2 %psum.14 = f32[]{:T(128)} all-reduce(f32[]{:T(128)S(6)} %select_n.252), channel_id=1, replica_groups=mesh['row'=32,'col'=16] {'row'}, use_global_device_ids=true, to_apply=%region_1.2 | all-reduce | flops 1 | bytes 8 | tf_op jit(solution)/shard_map/psum | solution.py:103
  340.2 40.2 %psum.15 = f32[]{:T(128)} all-reduce(f32[]{:T(128)} %psum.14), channel_id=1, replica_groups=mesh['row'=32,'col'=16] {'col'}, use_global_device_ids=true, to_apply=%region_2.3 | all-reduce | flops 1 | bytes 8 | tf_op jit(solution)/shard_map/psum | solution.py:103
  (103 shorter events, 41.1 us)
Async XLA Ops:
  0.6 110.1 %copy-start = (bf16[1,1,2,8,128,128]{5,4,3,2,1,0:T(8,128)(2,1)S(1)}, bf16[1,1,2,8,128,128]{5,4,3,2,1,0:T(8,128)(2,1)}, u32[]{:S(2)}) copy-start(bf16[1,1,2,8,128,128]{5,4,3,2,1,0:T(8,128)(2,1)} %param.4) | copy-start | bytes 1572868
  0.6 29.2 %collective-permute-start.12 = (s32[2,8]{1,0:T(2,128)}, s32[2,8]{1,0:T(2,128)S(1)}, u32[]{:S(2)}, u32[]{:S(2)}) collective-permute-start(s32[2,8]{1,0:T(2,128)} %bitcast.239), channel_id=1, source_target_pairs={{496,0},{0,16},{16,32},{32,48},{48,64},{64,80},{80,96},{96,112},{1... | collective-permute-start | bytes 200 | tf_op jit(solution)/shard_map/ppermute | solution.py:18
  5.5 27.3 %collective-permute-start.17 = (s32[2,8]{1,0:T(2,128)S(1)}, s32[2,8]{1,0:T(2,128)S(1)}, u32[]{:S(2)}, u32[]{:S(2)}) collective-permute-start(s32[2,8]{1,0:T(2,128)S(1)} %bitcast_add_fusion), channel_id=1, source_target_pairs={{496,0},{0,16},{16,32},{32,48},{48,64},{64,80},{80,96},{96,112},{1... | collective-permute-start | bytes 200 | tf_op jit(solution)/shard_map/ppermute | solution.py:18
  10.5 100.3 %collective-permute-start.22 = (bf16[2,8,128,128]{3,2,1,0:T(8,128)(2,1)S(1)}, bf16[2,8,128,128]{3,2,1,0:T(8,128)(2,1)S(1)}, u32[]{:S(2)}, u32[]{:S(2)}) collective-permute-start(bf16[2,8,128,128]{3,2,1,0:T(8,128)(2,1)S(1)} %bitcast_multiply_fusion), channel_id=1, source_target_pairs={{496,0},{0,16},{16,32},{32,48},{48,64},{64,80},{80,96},{96,112},{1... | collective-permute-start | bytes 1572872 | tf_op jit(solution)/shard_map/ppermute | solution.py:18
  13.4 95.4 %collective-permute-start.8 = (bf16[8,128,128]{2,1,0:T(8,128)(2,1)S(1)}, bf16[8,128,128]{2,1,0:T(8,128)(2,1)S(1)}, u32[]{:S(2)}, u32[]{:S(2)}) collective-permute-start(bf16[8,128,128]{2,1,0:T(8,128)(2,1)S(1)} %dynamic-slice_bitcast_fusion), channel_id=1, source_target_pairs={{15,0},{0,1},{1,2},{2,3},{3,4},{4,5},{5,6},{6,7},{7,8},{8,9},{9,10... | collective-permute-start | bytes 786440 | tf_op jit(solution)/shard_map/ppermute | solution.py:18
  17.6 2.7 collective-permute-start
  20.2 7.0 %collective-permute-start.4 = (s32[8]{0:T(128)S(1)}, s32[8]{0:T(128)S(1)}, u32[]{:S(2)}, u32[]{:S(2)}) collective-permute-start(s32[8]{0:T(128)S(1)} %fusion.58), channel_id=1, source_target_pairs={{15,0},{0,1},{1,2},{2,3},{3,4},{4,5},{5,6},{6,7},{7,8},{8,9},{9,10... | collective-permute-start | bytes 104 | tf_op jit(solution)/shard_map/ppermute | solution.py:18
  27.3 11.0 %collective-permute-start.1 = (s32[8]{0:T(128)S(1)}, s32[8]{0:T(128)S(1)}, u32[]{:S(2)}, u32[]{:S(2)}) collective-permute-start(s32[8]{0:T(128)S(1)} %broadcast_select_fusion.20), channel_id=1, source_target_pairs={{14,0},{15,1},{0,2},{1,3},{2,4},{3,5},{4,6},{5,7},{6,8},{7,9},{8,1... | collective-permute-start | bytes 104 | tf_op jit(solution)/shard_map/ppermute | solution.py:18
  29.9 11.5 %collective-permute-start.5 = (s32[8]{0:T(128)S(1)}, s32[8]{0:T(128)S(1)}, u32[]{:S(2)}, u32[]{:S(2)}) collective-permute-start(s32[8]{0:T(128)S(1)} %broadcast_select_fusion.19), channel_id=1, source_target_pairs={{14,0},{15,1},{0,2},{1,3},{2,4},{3,5},{4,6},{5,7},{6,8},{7,9},{8,1... | collective-permute-start | bytes 104 | tf_op jit(solution)/shard_map/ppermute | solution.py:18
  32.8 29.3 %collective-permute-start.13 = (s32[2,8]{1,0:T(2,128)S(1)}, s32[2,8]{1,0:T(2,128)S(1)}, u32[]{:S(2)}, u32[]{:S(2)}) collective-permute-start(s32[2,8]{1,0:T(2,128)S(1)} %broadcast_select_fusion.10), channel_id=1, source_target_pairs={{480,0},{496,16},{0,32},{16,48},{32,64},{48,80},{64,96},{80,112},{... | collective-permute-start | bytes 200 | tf_op jit(solution)/shard_map/ppermute | solution.py:18
  38.2 25.8 %collective-permute-start.18 = (s32[2,8]{1,0:T(2,128)S(1)}, s32[2,8]{1,0:T(2,128)S(1)}, u32[]{:S(2)}, u32[]{:S(2)}) collective-permute-start(s32[2,8]{1,0:T(2,128)S(1)} %broadcast_select_fusion.9), channel_id=1, source_target_pairs={{480,0},{496,16},{0,32},{16,48},{32,64},{48,80},{64,96},{80,112},{... | collective-permute-start | bytes 200 | tf_op jit(solution)/shard_map/ppermute | solution.py:18
  41.4 6.9 %collective-permute-start.2 = (s32[8]{0:T(128)S(1)}, s32[8]{0:T(128)S(1)}, u32[]{:S(2)}, u32[]{:S(2)}) collective-permute-start(s32[8]{0:T(128)S(1)} %broadcast_select_fusion.22), channel_id=1, source_target_pairs={{12,0},{13,1},{14,2},{15,3},{0,4},{1,5},{2,6},{3,7},{4,8},{5,9},{6... | collective-permute-start | bytes 104 | tf_op jit(solution)/shard_map/ppermute | solution.py:18
  48.3 6.4 %collective-permute-start.6 = (s32[8]{0:T(128)S(1)}, s32[8]{0:T(128)S(1)}, u32[]{:S(2)}, u32[]{:S(2)}) collective-permute-start(s32[8]{0:T(128)S(1)} %broadcast_select_fusion.21), channel_id=1, source_target_pairs={{12,0},{13,1},{14,2},{15,3},{0,4},{1,5},{2,6},{3,7},{4,8},{5,9},{6... | collective-permute-start | bytes 104 | tf_op jit(solution)/shard_map/ppermute | solution.py:18
  54.7 12.7 %collective-permute-start.3 = (s32[8]{0:T(128)S(1)}, s32[8]{0:T(128)S(1)}, u32[]{:S(2)}, u32[]{:S(2)}) collective-permute-start(s32[8]{0:T(128)S(1)} %broadcast_select_fusion.24), channel_id=1, source_target_pairs={{8,0},{9,1},{10,2},{11,3},{12,4},{13,5},{14,6},{15,7},{0,8},{1,9},... | collective-permute-start | bytes 104 | tf_op jit(solution)/shard_map/ppermute | solution.py:18
  62.1 8.4 %collective-permute-start.7 = (s32[8]{0:T(128)S(1)}, s32[8]{0:T(128)S(1)}, u32[]{:S(2)}, u32[]{:S(2)}) collective-permute-start(s32[8]{0:T(128)S(1)} %broadcast_select_fusion.23), channel_id=1, source_target_pairs={{8,0},{9,1},{10,2},{11,3},{12,4},{13,5},{14,6},{15,7},{0,8},{1,9},... | collective-permute-start | bytes 104 | tf_op jit(solution)/shard_map/ppermute | solution.py:18
  64.1 19.6 %collective-permute-start.14 = (s32[2,8]{1,0:T(2,128)S(1)}, s32[2,8]{1,0:T(2,128)S(1)}, u32[]{:S(2)}, u32[]{:S(2)}) collective-permute-start(s32[2,8]{1,0:T(2,128)S(1)} %broadcast_select_fusion.12), channel_id=1, source_target_pairs={{448,0},{464,16},{480,32},{496,48},{0,64},{16,80},{32,96},{48,112}... | collective-permute-start | bytes 200 | tf_op jit(solution)/shard_map/ppermute | solution.py:18
  67.3 19.2 %collective-permute-start.19 = (s32[2,8]{1,0:T(2,128)S(1)}, s32[2,8]{1,0:T(2,128)S(1)}, u32[]{:S(2)}, u32[]{:S(2)}) collective-permute-start(s32[2,8]{1,0:T(2,128)S(1)} %broadcast_select_fusion.11), channel_id=1, source_target_pairs={{448,0},{464,16},{480,32},{496,48},{0,64},{16,80},{32,96},{48,112}... | collective-permute-start | bytes 200 | tf_op jit(solution)/shard_map/ppermute | solution.py:18
  70.6 8.4 %collective-permute-start.28 = (s32[8]{0:T(128)S(1)}, s32[8]{0:T(128)S(1)}, u32[]{:S(2)}, u32[]{:S(2)}) collective-permute-start(s32[8]{0:T(128)S(1)} %get-tuple-element.4), channel_id=1, source_target_pairs={{1,0},{2,1},{3,2},{4,3},{5,4},{6,5},{7,6},{8,7},{9,8},{10,9},{11,1... | collective-permute-start | bytes 104 | tf_op jit(solution)/shard_map/ppermute | solution.py:18
  79.0 3.0 collective-permute-start.27
  82.0 9.1 %collective-permute-start.34 = (s32[8]{0:T(128)S(1)}, s32[8]{0:T(128)S(1)}, u32[]{:S(2)}, u32[]{:S(2)}) collective-permute-start(s32[8]{0:T(128)S(1)} %collective-permute-done.28), channel_id=1, source_target_pairs={{1,0},{2,1},{3,2},{4,3},{5,4},{6,5},{7,6},{8,7},{9,8},{10,9},{11,1... | collective-permute-start | bytes 104 | tf_op jit(solution)/shard_map/ppermute | solution.py:18
  83.7 9.9 %collective-permute-start.33 = (s32[8]{0:T(128)S(1)}, s32[8]{0:T(128)S(1)}, u32[]{:S(2)}, u32[]{:S(2)}) collective-permute-start(s32[8]{0:T(128)S(1)} %collective-permute-done.27), channel_id=1, source_target_pairs={{1,0},{2,1},{3,2},{4,3},{5,4},{6,5},{7,6},{8,7},{9,8},{10,9},{11,1... | collective-permute-start | bytes 104 | tf_op jit(solution)/shard_map/ppermute | solution.py:18
  86.6 13.0 %collective-permute-start.15 = (s32[2,8]{1,0:T(2,128)S(1)}, s32[2,8]{1,0:T(2,128)S(1)}, u32[]{:S(2)}, u32[]{:S(2)}) collective-permute-start(s32[2,8]{1,0:T(2,128)S(1)} %broadcast_select_fusion.14), channel_id=1, source_target_pairs={{384,0},{400,16},{416,32},{432,48},{448,64},{464,80},{480,96},{496... | collective-permute-start | bytes 200 | tf_op jit(solution)/shard_map/ppermute | solution.py:18
  91.1 12.8 %collective-permute-start.20 = (s32[2,8]{1,0:T(2,128)S(1)}, s32[2,8]{1,0:T(2,128)S(1)}, u32[]{:S(2)}, u32[]{:S(2)}) collective-permute-start(s32[2,8]{1,0:T(2,128)S(1)} %broadcast_select_fusion.13), channel_id=1, source_target_pairs={{384,0},{400,16},{416,32},{432,48},{448,64},{464,80},{480,96},{496... | collective-permute-start | bytes 200 | tf_op jit(solution)/shard_map/ppermute | solution.py:18
  93.6 3.0 collective-permute-start.40
  96.5 3.0 collective-permute-start.39
  99.5 22.5 %collective-permute-start.16 = (s32[2,8]{1,0:T(2,128)S(1)}, s32[2,8]{1,0:T(2,128)S(1)}, u32[]{:S(2)}, u32[]{:S(2)}) collective-permute-start(s32[2,8]{1,0:T(2,128)S(1)} %broadcast_select_fusion.16), channel_id=1, source_target_pairs={{256,0},{272,16},{288,32},{304,48},{320,64},{336,80},{352,96},{368... | collective-permute-start | bytes 200 | tf_op jit(solution)/shard_map/ppermute | solution.py:18
  104.0 18.1 %collective-permute-start.21 = (s32[2,8]{1,0:T(2,128)S(1)}, s32[2,8]{1,0:T(2,128)S(1)}, u32[]{:S(2)}, u32[]{:S(2)}) collective-permute-start(s32[2,8]{1,0:T(2,128)S(1)} %broadcast_select_fusion.15), channel_id=1, source_target_pairs={{256,0},{272,16},{288,32},{304,48},{320,64},{336,80},{352,96},{368... | collective-permute-start | bytes 200 | tf_op jit(solution)/shard_map/ppermute | solution.py:18
  108.8 11.2 %collective-permute-start.9 = (bf16[8,128,128]{2,1,0:T(8,128)(2,1)S(1)}, bf16[8,128,128]{2,1,0:T(8,128)(2,1)S(1)}, u32[]{:S(2)}, u32[]{:S(2)}) collective-permute-start(bf16[8,128,128]{2,1,0:T(8,128)(2,1)S(1)} %broadcast_select_fusion.5), channel_id=1, source_target_pairs={{14,0},{15,1},{0,2},{1,3},{2,4},{3,5},{4,6},{5,7},{6,8},{7,9},{8,1... | collective-permute-start | bytes 786440 | tf_op jit(solution)/shard_map/ppermute | solution.py:18
  110.9 36.3 %collective-permute-start.23 = (bf16[2,8,128,128]{3,2,1,0:T(8,128)(2,1)S(1)}, bf16[2,8,128,128]{3,2,1,0:T(8,128)(2,1)S(1)}, u32[]{:S(2)}, u32[]{:S(2)}) collective-permute-start(bf16[2,8,128,128]{3,2,1,0:T(8,128)(2,1)S(1)} %broadcast_select_fusion), channel_id=1, source_target_pairs={{480,0},{496,16},{0,32},{16,48},{32,64},{48,80},{64,96},{80,112},{... | collective-permute-start | bytes 1572872 | tf_op jit(solution)/shard_map/ppermute | solution.py:18
  120.1 21.6 %collective-permute-start.10 = (bf16[8,128,128]{2,1,0:T(8,128)(2,1)S(1)}, bf16[8,128,128]{2,1,0:T(8,128)(2,1)S(1)}, u32[]{:S(2)}, u32[]{:S(2)}) collective-permute-start(bf16[8,128,128]{2,1,0:T(8,128)(2,1)S(1)} %broadcast_select_fusion.6), channel_id=1, source_target_pairs={{12,0},{13,1},{14,2},{15,3},{0,4},{1,5},{2,6},{3,7},{4,8},{5,9},{6... | collective-permute-start | bytes 786440 | tf_op jit(solution)/shard_map/ppermute | solution.py:18
  122.1 8.8 %collective-permute-start.31 = (s32[2,8]{1,0:T(2,128)S(1)}, s32[2,8]{1,0:T(2,128)S(1)}, u32[]{:S(2)}, u32[]{:S(2)}) collective-permute-start(s32[2,8]{1,0:T(2,128)S(1)} %get-tuple-element.7), channel_id=1, source_target_pairs={{32,0},{48,16},{64,32},{80,48},{96,64},{112,80},{128,96},{144,112}... | collective-permute-start | bytes 200 | tf_op jit(solution)/shard_map/ppermute | solution.py:18
  127.9 6.1 %collective-permute-start.30 = (s32[2,8]{1,0:T(2,128)S(1)}, s32[2,8]{1,0:T(2,128)S(1)}, u32[]{:S(2)}, u32[]{:S(2)}) collective-permute-start(s32[2,8]{1,0:T(2,128)S(1)} %get-tuple-element.6), channel_id=1, source_target_pairs={{32,0},{48,16},{64,32},{80,48},{96,64},{112,80},{128,96},{144,112}... | collective-permute-start | bytes 200 | tf_op jit(solution)/shard_map/ppermute | solution.py:18
  134.1 15.5 %collective-permute-start.37 = (s32[2,8]{1,0:T(2,128)S(1)}, s32[2,8]{1,0:T(2,128)S(1)}, u32[]{:S(2)}, u32[]{:S(2)}) collective-permute-start(s32[2,8]{1,0:T(2,128)S(1)} %collective-permute-done.31), channel_id=1, source_target_pairs={{32,0},{48,16},{64,32},{80,48},{96,64},{112,80},{128,96},{144,112}... | collective-permute-start | bytes 200 | tf_op jit(solution)/shard_map/ppermute | solution.py:18
  138.9 10.6 %collective-permute-start.36 = (s32[2,8]{1,0:T(2,128)S(1)}, s32[2,8]{1,0:T(2,128)S(1)}, u32[]{:S(2)}, u32[]{:S(2)}) collective-permute-start(s32[2,8]{1,0:T(2,128)S(1)} %collective-permute-done.30), channel_id=1, source_target_pairs={{32,0},{48,16},{64,32},{80,48},{96,64},{112,80},{128,96},{144,112}... | collective-permute-start | bytes 200 | tf_op jit(solution)/shard_map/ppermute | solution.py:18
  141.7 19.9 %collective-permute-start.11 = (bf16[8,128,128]{2,1,0:T(8,128)(2,1)S(1)}, bf16[8,128,128]{2,1,0:T(8,128)(2,1)S(1)}, u32[]{:S(2)}, u32[]{:S(2)}) collective-permute-start(bf16[8,128,128]{2,1,0:T(8,128)(2,1)S(1)} %broadcast_select_fusion.7), channel_id=1, source_target_pairs={{8,0},{9,1},{10,2},{11,3},{12,4},{13,5},{14,6},{15,7},{0,8},{1,9},... | collective-permute-start | bytes 786440 | tf_op jit(solution)/shard_map/ppermute | solution.py:18
  147.2 20.0 %collective-permute-start.24 = (bf16[2,8,128,128]{3,2,1,0:T(8,128)(2,1)S(1)}, bf16[2,8,128,128]{3,2,1,0:T(8,128)(2,1)S(1)}, u32[]{:S(2)}, u32[]{:S(2)}) collective-permute-start(bf16[2,8,128,128]{3,2,1,0:T(8,128)(2,1)S(1)} %broadcast_select_fusion.1), channel_id=1, source_target_pairs={{448,0},{464,16},{480,32},{496,48},{0,64},{16,80},{32,96},{48,112}... | collective-permute-start | bytes 1572872 | tf_op jit(solution)/shard_map/ppermute | solution.py:18
  149.6 8.8 %collective-permute-start.43 = (s32[2,8]{1,0:T(2,128)S(1)}, s32[2,8]{1,0:T(2,128)S(1)}, u32[]{:S(2)}, u32[]{:S(2)}) collective-permute-start(s32[2,8]{1,0:T(2,128)S(1)} %collective-permute-done.37), channel_id=1, source_target_pairs={{32,0},{48,16},{64,32},{80,48},{96,64},{112,80},{128,96},{144,112}... | collective-permute-start | bytes 200 | tf_op jit(solution)/shard_map/ppermute | solution.py:18
  155.7 5.8 %collective-permute-start.42 = (s32[2,8]{1,0:T(2,128)S(1)}, s32[2,8]{1,0:T(2,128)S(1)}, u32[]{:S(2)}, u32[]{:S(2)}) collective-permute-start(s32[2,8]{1,0:T(2,128)S(1)} %collective-permute-done.36), channel_id=1, source_target_pairs={{32,0},{48,16},{64,32},{80,48},{96,64},{112,80},{128,96},{144,112}... | collective-permute-start | bytes 200 | tf_op jit(solution)/shard_map/ppermute | solution.py:18
  161.6 8.8 %collective-permute-start.29 = (bf16[8,128,128]{2,1,0:T(8,128)(2,1)S(1)}, bf16[8,128,128]{2,1,0:T(8,128)(2,1)S(1)}, u32[]{:S(2)}, u32[]{:S(2)}) collective-permute-start(bf16[8,128,128]{2,1,0:T(8,128)(2,1)S(1)} %broadcast_select_fusion.8), channel_id=1, source_target_pairs={{1,0},{2,1},{3,2},{4,3},{5,4},{6,5},{7,6},{8,7},{9,8},{10,9},{11,1... | collective-permute-start | bytes 786440 | tf_op jit(solution)/shard_map/ppermute | solution.py:18
  167.3 26.0 %collective-permute-start.25 = (bf16[2,8,128,128]{3,2,1,0:T(8,128)(2,1)S(1)}, bf16[2,8,128,128]{3,2,1,0:T(8,128)(2,1)S(1)}, u32[]{:S(2)}, u32[]{:S(2)}) collective-permute-start(bf16[2,8,128,128]{3,2,1,0:T(8,128)(2,1)S(1)} %broadcast_select_fusion.2), channel_id=1, source_target_pairs={{384,0},{400,16},{416,32},{432,48},{448,64},{464,80},{480,96},{496... | collective-permute-start | bytes 1572872 | tf_op jit(solution)/shard_map/ppermute | solution.py:18
  170.5 6.1 %collective-permute-start.35 = (bf16[8,128,128]{2,1,0:T(8,128)(2,1)S(1)}, bf16[8,128,128]{2,1,0:T(8,128)(2,1)S(1)}, u32[]{:S(2)}, u32[]{:S(2)}) collective-permute-start(bf16[8,128,128]{2,1,0:T(8,128)(2,1)S(1)} %collective-permute-done.29), channel_id=1, source_target_pairs={{1,0},{2,1},{3,2},{4,3},{5,4},{6,5},{7,6},{8,7},{9,8},{10,9},{11,1... | collective-permute-start | bytes 786440 | tf_op jit(solution)/shard_map/ppermute | solution.py:18
  176.6 21.5 %collective-permute-start.41 = (bf16[8,128,128]{2,1,0:T(8,128)(2,1)S(1)}, bf16[8,128,128]{2,1,0:T(8,128)(2,1)S(1)}, u32[]{:S(2)}, u32[]{:S(2)}) collective-permute-start(bf16[8,128,128]{2,1,0:T(8,128)(2,1)S(1)} %collective-permute-done.35), channel_id=1, source_target_pairs={{1,0},{2,1},{3,2},{4,3},{5,4},{6,5},{7,6},{8,7},{9,8},{10,9},{11,1... | collective-permute-start | bytes 786440 | tf_op jit(solution)/shard_map/ppermute | solution.py:18
  193.4 30.9 %collective-permute-start.26 = (bf16[2,8,128,128]{3,2,1,0:T(8,128)(2,1)S(1)}, bf16[2,8,128,128]{3,2,1,0:T(8,128)(2,1)S(1)}, u32[]{:S(2)}, u32[]{:S(2)}) collective-permute-start(bf16[2,8,128,128]{3,2,1,0:T(8,128)(2,1)S(1)} %broadcast_select_fusion.3), channel_id=1, source_target_pairs={{256,0},{272,16},{288,32},{304,48},{320,64},{336,80},{352,96},{368... | collective-permute-start | bytes 1572872 | tf_op jit(solution)/shard_map/ppermute | solution.py:18
  224.3 16.3 %collective-permute-start.32 = (bf16[2,8,128,128]{3,2,1,0:T(8,128)(2,1)S(1)}, bf16[2,8,128,128]{3,2,1,0:T(8,128)(2,1)S(1)}, u32[]{:S(2)}, u32[]{:S(2)}) collective-permute-start(bf16[2,8,128,128]{3,2,1,0:T(8,128)(2,1)S(1)} %broadcast_select_fusion.4), channel_id=1, source_target_pairs={{32,0},{48,16},{64,32},{80,48},{96,64},{112,80},{128,96},{144,112}... | collective-permute-start | bytes 1572872 | tf_op jit(solution)/shard_map/ppermute | solution.py:18
  240.7 15.4 %collective-permute-start.38 = (bf16[2,8,128,128]{3,2,1,0:T(8,128)(2,1)S(1)}, bf16[2,8,128,128]{3,2,1,0:T(8,128)(2,1)S(1)}, u32[]{:S(2)}, u32[]{:S(2)}) collective-permute-start(bf16[2,8,128,128]{3,2,1,0:T(8,128)(2,1)S(1)} %collective-permute-done.32), channel_id=1, source_target_pairs={{32,0},{48,16},{64,32},{80,48},{96,64},{112,80},{128,96},{144,112}... | collective-permute-start | bytes 1572872 | tf_op jit(solution)/shard_map/ppermute | solution.py:18
  256.1 16.0 %collective-permute-start.44 = (bf16[2,8,128,128]{3,2,1,0:T(8,128)(2,1)S(1)}, bf16[2,8,128,128]{3,2,1,0:T(8,128)(2,1)S(1)}, u32[]{:S(2)}, u32[]{:S(2)}) collective-permute-start(bf16[2,8,128,128]{3,2,1,0:T(8,128)(2,1)S(1)} %collective-permute-done.38), channel_id=1, source_target_pairs={{32,0},{48,16},{64,32},{80,48},{96,64},{112,80},{128,96},{144,112}... | collective-permute-start | bytes 1572872 | tf_op jit(solution)/shard_map/ppermute | solution.py:18
